TPU v7x, 32 devices: a whole 2x2x4 slice. The times are simulated.
32 devices in a mesh: seq: 16 (over z, y, x), head: 2 (over core).
Axes of the slice: x: 2, y: 2, z: 4, core: 2. Of those that a mesh axis runs over, the one named last changes fastest.
Arguments:
- queries: bfloat16 [2048, 32, 128], P('seq', 'head'), may hold values from -6 to 6
- key_vectors: bfloat16 [2048, 32, 128], P('seq', 'head'), may hold values from -6 to 6
- values: bfloat16 [2048, 32, 128], P('seq', 'head'), may hold values from -6 to 6
- out_grad: bfloat16 [2048, 32, 128], P('seq', 'head'), may hold values from -6 to 6
- hidden_in: bfloat16 [2048, 2048], P('seq'), may hold values from -6 to 6
- decay_weight: bfloat16 [2048, 32], P(None, 'head'), may hold values from -0.125 to 0.125
- write_weight: bfloat16 [2048, 32], P(None, 'head'), may hold values from -0.125 to 0.125
- decay_bias: float32 [32], P('head'), may hold values from -2 to 2
- decay_log: float32 [32], P('head'), may hold values from -11 to -2
- write_bias: float32 [32], P('head'), may hold values from -9 to 0
- start_state: float32 [16, 32, 128, 128], P('seq', 'head'), may hold values from -4 to 4
Outputs:
- grad_queries: bfloat16 [2048, 32, 128], P('seq', 'head')
- grad_keys: bfloat16 [2048, 32, 128], P('seq', 'head')
- grad_values: bfloat16 [2048, 32, 128], P('seq', 'head')
- grad_hidden: bfloat16 [2048, 2048], P('seq', 'head')
- grad_decay_weight: float32 [2048, 32], P(None, 'head')
- grad_write_weight: float32 [2048, 32], P(None, 'head')
All inputs are finite; a program needn't handle non-finite values.
Results may differ from a plain program's by a relative error of at most 0.014.
Values may be sent and summed in bfloat16 or wider, within the bound.
A program may use at most 128 MiB of HBM per device.

v0:
```python
from functools import partial

import jax
import jax.numpy as jnp
from jax import lax
from jax.sharding import PartitionSpec as P

EPSILON = 1e-06
PRECISION_MAXIMUM = lax.Precision.HIGHEST


def prefix(part, axis, combine, identity):
    count = lax.axis_size(axis)
    place = lax.axis_index(axis)
    ahead = count - 1 - place
    gathered = jax.tree.map(lambda a: lax.all_gather(a, axis), part)
    state = jax.tree.map(lambda a, e: jnp.zeros_like(a) + jnp.asarray(e, a.dtype), part, identity)

    def one(step, state):
        source = count - 1 - step
        return combine(
            state, jax.tree.map(lambda a: lax.dynamic_index_in_dim(a, source, 0, False), gathered)
        )

    return lax.fori_loop(0, ahead, one, state)


def block_forward(
    decay_log,
    decay_bias,
    write_bias,
    queries,
    key_vectors,
    values,
    decay_logit,
    write_logit,
    initial_state,
):
    normalized_queries = queries * lax.rsqrt(
        jnp.sum(queries * queries, axis=-1, keepdims=True) + EPSILON
    )
    normalized_keys = key_vectors * lax.rsqrt(
        jnp.sum(key_vectors * key_vectors, axis=-1, keepdims=True) + EPSILON
    )
    write_rate = jax.nn.sigmoid(write_logit + write_bias)
    log_decay = -jnp.exp(decay_log) * jax.nn.softplus(decay_logit + decay_bias)
    log_prefix = jnp.cumsum(log_decay, axis=0).T
    block_size = queries.shape[0]
    positions = jnp.arange(block_size, dtype=jnp.int32)
    lower_mask = positions[:, None] >= positions[None, :]
    strict_mask = positions[:, None] > positions[None, :]
    log_gaps = jnp.where(lower_mask, log_prefix[:, :, None] - log_prefix[:, None, :], 0.0)
    decay_ratio = jnp.where(lower_mask, jnp.exp(log_gaps), 0.0)
    key_gram = jnp.einsum(
        "ihk,jhk->hij", normalized_keys, normalized_keys, precision=PRECISION_MAXIMUM
    )
    coupling = jnp.where(strict_mask, write_rate.T[:, :, None] * decay_ratio * key_gram, 0.0)
    unit_lower = coupling + jnp.eye(block_size, dtype=coupling.dtype)
    cumulative_decay = jnp.exp(log_prefix)
    keys_against_state = jnp.einsum(
        "dlu,lux->ldx", normalized_keys, initial_state, precision=PRECISION_MAXIMUM
    )
    right_side = write_rate.T[:, :, None] * (
        jnp.swapaxes(values, 0, 1) - cumulative_decay[:, :, None] * keys_against_state
    )
    value_updates = jax.scipy.linalg.solve_triangular(
        unit_lower, right_side, lower=True, unit_diagonal=True
    )
    query_keys = decay_ratio * jnp.einsum(
        "ihk,jhk->hij", normalized_queries, normalized_keys, precision=PRECISION_MAXIMUM
    )
    layer_outputs = cumulative_decay[:, :, None] * jnp.einsum(
        "dlu,lux->ldx", normalized_queries, initial_state, precision=PRECISION_MAXIMUM
    )
    layer_outputs = layer_outputs + jnp.einsum(
        "hij,hjv->hiv", query_keys, value_updates, precision=PRECISION_MAXIMUM
    )
    final_decay_weights = decay_ratio[:, -1, :]
    final_state = cumulative_decay[:, -1][:, None, None] * initial_state + jnp.einsum(
        "zg,gzi,zgq->ziq",
        final_decay_weights,
        normalized_keys,
        value_updates,
        precision=PRECISION_MAXIMUM,
    )
    return (jnp.swapaxes(layer_outputs, 0, 1), final_state)


def combine_maps(earlier, later):
    offset = later[0] + jnp.einsum(
        "hab,hbv->hav", later[1], earlier[0], precision=PRECISION_MAXIMUM
    )
    linear = jnp.einsum("hab,hbc->hac", later[1], earlier[1], precision=PRECISION_MAXIMUM)
    return (offset, linear)


def shards(
    queries,
    key_vectors,
    values,
    out_grad,
    hidden_in,
    decay_weight,
    write_weight,
    decay_bias,
    decay_log,
    write_bias,
    start_state,
):
    decay_logit = jnp.dot(hidden_in, decay_weight, preferred_element_type=jnp.float32)
    write_logit = jnp.dot(hidden_in, write_weight, preferred_element_type=jnp.float32)
    query_full = queries.astype(jnp.float32)
    key_full = key_vectors.astype(jnp.float32)
    value_full = values.astype(jnp.float32)
    initial_state = start_state[0]
    forward = partial(block_forward, decay_log, decay_bias, write_bias)
    primal, pullback = jax.vjp(
        forward, query_full, key_full, value_full, decay_logit, write_logit, initial_state
    )
    layer_outputs, final_state = primal
    local_grads = pullback((out_grad.astype(jnp.float32), jnp.zeros_like(final_state)))
    head_count = initial_state.shape[0]
    key_width = initial_state.shape[1]
    identity_block = jnp.broadcast_to(
        jnp.eye(key_width, dtype=jnp.float32), (head_count, key_width, key_width)
    )
    no_values = jnp.zeros(query_full.shape, jnp.float32)
    _, propagator = forward(
        query_full, key_full, no_values, decay_logit, write_logit, identity_block
    )
    transfer = jnp.swapaxes(propagator, 1, 2)
    summary = prefix(
        (local_grads[5], transfer),
        "seq",
        combine_maps,
        (jnp.zeros_like(initial_state), identity_block),
    )
    carry_grads = pullback((jnp.zeros_like(layer_outputs), summary[0]))
    totals = [local_grads[member] + carry_grads[member] for member in range(5)]
    decay_grads = totals[3].astype(jnp.bfloat16)
    write_grads = totals[4].astype(jnp.bfloat16)
    weight_terms = (
        jnp.einsum("td,th->dh", hidden_in, decay_grads, preferred_element_type=jnp.float32),
        jnp.einsum("td,th->dh", hidden_in, write_grads, preferred_element_type=jnp.float32),
    )
    grad_decay_weight, grad_write_weight = lax.psum((weight_terms[0], weight_terms[1]), "seq")
    partial_terms = jnp.einsum(
        "th,dh->td", decay_grads, decay_weight, preferred_element_type=jnp.float32
    )
    partial_terms = partial_terms + jnp.einsum(
        "th,dh->td", write_grads, write_weight, preferred_element_type=jnp.float32
    )
    grad_hidden = lax.psum_scatter(
        partial_terms.astype(jnp.bfloat16), "head", scatter_dimension=1, tiled=True
    )
    return (
        totals[0].astype(jnp.bfloat16),
        totals[1].astype(jnp.bfloat16),
        totals[2].astype(jnp.bfloat16),
        grad_hidden,
        grad_decay_weight,
        grad_write_weight,
    )


def solution(mesh):
    placed = (
        P("seq", "head", None),
        P("seq", "head", None),
        P("seq", "head", None),
        P("seq", "head", None),
        P("seq", None),
        P(None, "head"),
        P(None, "head"),
        P("head"),
        P("head"),
        P("head"),
        P("seq", "head", None, None),
    )
    return jax.shard_map(
        shards,
        mesh=mesh,
        in_specs=placed,
        out_specs=(
            P("seq", "head", None),
            P("seq", "head", None),
            P("seq", "head", None),
            P("seq", "head"),
            P(None, "head"),
            P(None, "head"),
        ),
        check_vma=False,
    )
```

profile of v0, /device:TPU:0, one launch (start us, length us, event | category | flops | bytes accessed | tf_op | source)
XLA Modules:
  0.0 814.2 jit_solution(14661135302371511442)
XLA Ops:
  16.2 157.9 %custom-call.10 = f32[16,1,128,128]{2,3,1,0:T(8,128)S(1)} custom-call(f32[16,1,128,128]{3,2,1,0:T(8,128)} %get-tuple-element.158), custom_call_target="InvertDiagBlocksLowerTriangular" | custom-call | tf_op jit(solution)/shard_map/jvp(jit(_solve_triangular))/vmap()/triangular_solve/custom-call.1 | solution.py:66
  174.2 3.4 fusion.15
  177.6 4.1 fusion.81
  181.7 3.3 fusion.163
  185.0 4.4 fusion.53
  189.4 3.3 convolution_bitcast_fusion.4
  195.0 2.4 fusion.86
  200.1 3.8 fusion.36
  203.8 5.7 fusion.71
  209.5 3.4 fusion.11
  213.9 2.4 convolution_add_fusion.4
  226.7 3.3 convolution_add_fusion.3
  230.3 2.9 fusion.64
  235.5 3.6 multiply_reduce_fusion.5
  239.1 3.9 fusion.232
  245.3 3.6 fusion.38
  249.0 2.5 fusion.37
  251.4 4.9 convolution_bitcast_fusion.3
  256.3 160.1 %all-gather.5.cloned.1.call-done = f32[256,128,128]{2,1,0:T(8,128)} async-done(((f32[16,128,128]{2,1,0:T(8,128)}), f32[256,128,128]{2,1,0:T(8,128)}) %all-gather.5.cloned.1.call-update) | async-done | bytes 16777232 | tf_op jit(solution)/shard_map/all_gather | solution.py:16
  416.4 192.0 %all-gather.7.cloned.1.call-done = f32[256,128,128]{2,1,0:T(8,128)} async-done(((f32[16,128,128]{2,1,0:T(8,128)}), f32[256,128,128]{2,1,0:T(8,128)}) %all-gather.7.cloned.1.call-update) | async-done | bytes 16777232 | tf_op jit(solution)/shard_map/all_gather | solution.py:16
  608.5 42.7 %while.14 = (s32[]{:T(128)}, f32[16,128,128]{2,1,0:T(8,128)S(1)}, s32[]{:T(128)}, f32[16,16,128,128]{3,2,1,0:T(8,128)}, f32[16,16,128,128]{3,2,1,0:T(8,128)}, /*index=5*/s32[]{:T(128)}, s32[]{:T(128)}, s32[]{:T(128)}, s32[]{:T(128)}) while((s32[]{:T(128)}, f32[16,128,128]{2,1,0:T(8,128)S(1)}, s32[]{:T(128)}, f32[16,16,128,128]{3,2,1,0:T(8,128)}, ...), condition=%wide.region_7.10_spmd, body=%wide.region_6.9_spmd.sunk | while | flops 402915328 | bytes 6292627 | solution.py:25
  608.6 2.7 convolution_add_fusion.8
  611.4 2.7 convolution_add_fusion.8
  614.2 2.7 convolution_add_fusion.8
  617.1 2.7 convolution_add_fusion.8
  619.9 2.7 convolution_add_fusion.8
  622.8 2.7 convolution_add_fusion.8
  625.6 2.7 convolution_add_fusion.8
  628.4 2.8 convolution_add_fusion.8
  631.3 2.7 convolution_add_fusion.8
  634.1 2.7 convolution_add_fusion.8
  637.0 2.7 convolution_add_fusion.8
  639.8 2.7 convolution_add_fusion.8
  642.6 2.7 convolution_add_fusion.8
  645.4 2.7 convolution_add_fusion.8
  648.3 2.7 convolution_add_fusion.8
  653.1 3.3 convolution_add_fusion.2
  656.4 3.5 fusion.233
  660.0 3.6 fusion.47
  663.6 3.9 fusion.43
  667.5 2.5 fusion.42
  671.2 3.4 fusion.61
  674.9 3.7 convolution_bitcast_fusion.2
  678.7 6.0 multiply_select_fusion
  691.5 4.2 fusion.32
  695.8 4.2 fusion.68
  703.8 90.5 %all-reduce.7.cloned.1.call-done = (f32[2048,16]{0,1:T(8,128)}, f32[2048,16]{0,1:T(8,128)}) async-done(((f32[2048,16]{0,1:T(8,128)}, f32[2048,16]{0,1:T(8,128)}), (f32[2048,16]{0,1:T(8,128)}, f32[2048,16]{0,1:T(8,128)})) %all-reduce.7.cloned.1.call-update) | async-done | bytes 262160 | tf_op jit(solution)/shard_map/psum | solution.py:146
  794.3 9.7 %reduce-scatter.2.cloned.1.call-done = bf16[128,1024]{1,0:T(8,128)(2,1)} async-done(((bf16[128,2048]{1,0:T(8,128)(2,1)}), bf16[128,1024]{1,0:T(8,128)(2,1)}) %reduce-scatter.2.cloned.1.call-update) | async-done | bytes 262160 | tf_op jit(solution)/shard_map/reduce_scatter | solution.py:153
  (125 shorter events, 48.9 us)
Async XLA Ops:
  7.2 1.0 copy-start
  7.2 177.8 %copy-start.3 = (f32[1,16,128,128]{3,2,1,0:T(8,128)S(1)}, f32[1,16,128,128]{3,2,1,0:T(8,128)}, u32[]{:S(2)}) copy-start(f32[1,16,128,128]{3,2,1,0:T(8,128)} %param.27) | copy-start | bytes 3145732
  7.2 409.2 %all-gather.5.cloned.1.call-start = ((), (), s32[]{:S(2)}) async-start(), calls=%async_computation.2 | async-start | bytes 17825792 | tf_op jit(solution)/shard_map/all_gather | solution.py:16
  13.2 3.0 copy-start.14
  174.1 68.8 %copy-start.1 = (f32[16,1,128,128]{2,3,1,0:T(8,128)}, f32[16,1,128,128]{2,3,1,0:T(8,128)S(1)}, u32[]{:S(2)}) copy-start(f32[16,1,128,128]{2,3,1,0:T(8,128)S(1)} %custom-call.10) | copy-start | bytes 3145732
  177.6 15.0 %copy-start.15 = (f32[16,128,128]{2,1,0:T(8,128)}, f32[16,128,128]{2,1,0:T(8,128)S(1)}, u32[]{:S(2)}) copy-start(f32[16,128,128]{2,1,0:T(8,128)S(1)} %fusion.15) | copy-start | bytes 3145732
  181.7 7.7 copy-start.5
  195.0 25.1 %copy-start.9 = (bf16[128,16,128]{0,2,1:T(8,128)(2,1)S(1)}, bf16[128,16,128]{0,2,1:T(8,128)(2,1)}, u32[]{:S(2)}) copy-start(bf16[128,16,128]{0,2,1:T(8,128)(2,1)} %copy.207) | copy-start | bytes 1572868
  195.0 25.1 %copy-start.17 = (bf16[128,16,128]{2,1,0:T(8,128)(2,1)S(1)}, bf16[128,16,128]{2,1,0:T(8,128)(2,1)}, u32[]{:S(2)}) copy-start(bf16[128,16,128]{2,1,0:T(8,128)(2,1)} %param.20) | copy-start | bytes 1572868
  203.8 16.3 %copy-start.16 = (f32[128,16,128]{0,2,1:T(8,128)}, f32[128,16,128]{0,2,1:T(8,128)S(1)}, u32[]{:S(2)}) copy-start(f32[128,16,128]{0,2,1:T(8,128)S(1)} %fusion.36) | copy-start | bytes 3145732
  212.9 1.0 copy-start.10
  216.4 3.7 copy-start.12
  217.6 1.0 copy-start.11
  222.5 385.9 %all-gather.7.cloned.1.call-start = ((), (), s32[]{:S(2)}) async-start(), calls=%async_computation.3 | async-start | bytes 17825792 | tf_op jit(solution)/shard_map/all_gather | solution.py:16
  230.0 564.2 %all-reduce.7.cloned.1.call-start = ((), (), s32[]{:S(2)}) async-start(), calls=%async_computation.4 | async-start | bytes 524288 | tf_op jit(solution)/shard_map/psum | solution.py:146
  245.3 3.7 copy-start.18
  651.2 18.8 %copy-start.2 = (f32[16,1,128,128]{2,3,1,0:T(8,128)S(1)}, f32[16,1,128,128]{2,3,1,0:T(8,128)}, u32[]{:S(2)}) copy-start(f32[16,1,128,128]{2,3,1,0:T(8,128)} %copy-done.1) | copy-start | bytes 3145732
  651.2 20.0 %copy-start.6 = (f32[16,128,128]{2,1,0:T(8,128)S(1)}, f32[16,128,128]{2,1,0:T(8,128)}, u32[]{:S(2)}) copy-start(f32[16,128,128]{2,1,0:T(8,128)} %copy-done.5) | copy-start | bytes 3145732
  651.2 20.0 %copy-start.7 = (f32[16,128,128]{2,1,0:T(8,128)S(1)}, f32[16,128,128]{2,1,0:T(8,128)}, u32[]{:S(2)}) copy-start(f32[16,128,128]{2,1,0:T(8,128)} %fusion.163) | copy-start | bytes 3145732
  651.2 23.4 %copy-start.4 = (f32[1,16,128,128]{3,2,1,0:T(8,128)S(1)}, f32[1,16,128,128]{3,2,1,0:T(8,128)}, u32[]{:S(2)}) copy-start(f32[1,16,128,128]{3,2,1,0:T(8,128)} %param.27) | copy-start | bytes 3145732
  663.5 3.9 copy-start.19
  663.6 24.4 %copy-start.21 = (bf16[2048,16]{0,1:T(8,128)(2,1)S(1)}, bf16[2048,16]{0,1:T(8,128)(2,1)}, u32[]{:S(2)}) copy-start(bf16[2048,16]{0,1:T(8,128)(2,1)} %param.22) | copy-start | bytes 196612
  667.5 22.9 %copy-start.20 = (bf16[2048,16]{0,1:T(8,128)(2,1)S(1)}, bf16[2048,16]{0,1:T(8,128)(2,1)}, u32[]{:S(2)}) copy-start(bf16[2048,16]{0,1:T(8,128)(2,1)} %param.23) | copy-start | bytes 196612
  671.2 7.3 copy-start.13
  674.9 20.9 %copy-start.8 = (f32[16,128,128]{2,1,0:T(8,128)S(1)}, f32[16,128,128]{2,1,0:T(8,128)}, u32[]{:S(2)}) copy-start(f32[16,128,128]{2,1,0:T(8,128)} %fusion.163) | copy-start | bytes 3145732
  690.1 113.9 %reduce-scatter.2.cloned.1.call-start = ((), (), s32[]{:S(2)}) async-start(), calls=%async_computation.1 | async-start | bytes 786432 | tf_op jit(solution)/shard_map/reduce_scatter | solution.py:153
Sparse Core Ops, SparseCore 0:
  222.6 193.7 all-gather.4
  419.1 189.1 all-gather.6
  690.2 104.0 all-reduce.6
  796.9 6.9 reduce-scatter.1
where the time goes:
time: 822 us; the launch traced here: 814 us
  waiting for transfers between devices  452 us (55%)
  other arithmetic  174 us (21%)
  matrix products  154 us (19%)
  local copies, waits for them, and re-layouts  17.9 us (2%)
  between operations  14.8 us (2%)
    all_gather x2, waiting for transfers between devices, prefix(): gathered = jax.tree.map(lambda a: lax.all_gather(a, axis), part)  352 us
    another operation x4, other arithmetic, block_forward(): jax.scipy.linalg.solve_triangular(unit_lower, right_side, lower=True, uni...  158 us
    psum x1, waiting for transfers between devices, shards(): lax.psum((weight_terms[0], weight_terms[1]), 'seq')  90.5 us
    dot_general x15, matrix products, combine_maps(): jnp.einsum('hab,hbv->hav', later[1], earlier[0], precision=PRECISION_MAXI...  40.6 us
    dot_general x5, matrix products, block_forward(): jnp.einsum('ihk,jhk->hij', normalized_queries, normalized_keys, precision...  21.2 us
  transfers between devices with their start and end apart: 4, of which 4 were waited for; matrix products, arithmetic and copies ran while one was open for 6% of the time, Pallas kernels for 0%

commit v1 on v0

v1 whole, which is shorter than its diff:
```python
from functools import partial

import jax
import jax.numpy as jnp
from jax import lax
from jax.experimental import pallas as pl
from jax.experimental.pallas import tpu as pltpu
from jax.sharding import PartitionSpec as P

EPSILON = 1e-06
HI = lax.Precision.HIGHEST
F32 = jnp.float32
BF = jnp.bfloat16


def mm(a, b, ca=1, cb=0):
    return lax.dot_general(
        a.astype(BF), b.astype(BF), (((ca,), (cb,)), ((), ())), preferred_element_type=F32
    )


def unit(x):
    r = lax.rsqrt(jnp.sum(x * x, axis=1, keepdims=True) + EPSILON)
    return x * r, r


def unit_back(d, n, r):
    return r * (d - n * jnp.sum(n * d, axis=1, keepdims=True))


def indices(c):
    row = lax.broadcasted_iota(jnp.int32, (c, c), 0)
    col = lax.broadcasted_iota(jnp.int32, (c, c), 1)
    return row, col


def local_head(q, k, v, do, s0, rows):
    c = q.shape[0]
    row, col = indices(c)
    cols = rows.T
    g_col, beta = cols[:, 0:1], cols[:, 1:2]
    g_row = rows[0:1, :]
    g_last = g_row[:, c - 1 : c]
    cd = jnp.exp(g_col)
    to_end = jnp.exp(g_last - g_col)
    lower = row >= col
    gamma = jnp.where(lower, jnp.exp(jnp.where(lower, g_col - g_row, 0.0)), 0.0)
    gamma_strict = jnp.where(row > col, gamma, 0.0)
    qn, rq = unit(q.astype(F32))
    kn, _ = unit(k.astype(F32))
    qb, kb, sb = qn.astype(BF), kn.astype(BF), s0.astype(BF)
    gram = gamma_strict * mm(kb, kb, 1, 1)
    p = gamma * mm(qb, kb, 1, 1)
    z = v.astype(F32) - cd * mm(kb, sb)
    a = beta * gram
    inv = jnp.where(row == col, 1.0, jnp.where((row ^ col) == 1, -a, 0.0))
    level = 1
    while (2 << level) <= c:
        low, high = row >> level, col >> level
        band = jnp.where(((low ^ high) == 1), a, 0.0)
        inv = inv - mm(mm(inv, band), inv)
        level += 1
    ib = inv.astype(BF)
    ub = mm(ib, beta * z).astype(BF)
    ptdo = mm(p, do, 0, 0)
    w0 = mm(ib, ptdo, 0, 0)
    nb = mm(ib, to_end * kn, 0, 0).astype(BF)
    bck = ((beta * cd) * kn).astype(BF)
    off = mm(cd * qn, do, 0, 0) - mm(bck, w0, 0, 0)
    tt = mm(bck, nb, 0, 0)
    dp = mm(do, ub, 1, 1)
    dos = cd * mm(do, sb, 1, 1)
    gdp = (gamma * dp).astype(BF)
    dq = unit_back(dos + mm(gdp, kb), qn, rq)
    dk0 = mm(gdp, qb, 0, 0)
    t = dp * p
    dg0 = jnp.sum((t + dos * qn).T, axis=0, keepdims=True) - jnp.sum(t, axis=0, keepdims=True)
    return dq, ub, w0, nb, tt, off, z, gram, gamma_strict, dk0, dg0


def carry_head(k, v, s0, e, rows, ub, w0, nb, z, gram, gamma_strict, dk0, dg0):
    c = k.shape[0]
    row, col = indices(c)
    cols = rows.T
    g_col, beta = cols[:, 0:1], cols[:, 1:2]
    g_last = rows[0:1, c - 1 : c]
    cd = jnp.exp(g_col)
    to_end = jnp.exp(g_last - g_col)
    kn, rk = unit(k.astype(F32))
    kb = kn.astype(BF)
    w = w0 + mm(nb, e)
    wb = w.astype(BF)
    dv = beta * w
    da = -mm(wb, ub, 1, 1)
    ws = mm(wb, s0, 1, 1)
    ue = to_end * mm(ub, e, 1, 1)
    dkk = (beta * gamma_strict * da).astype(BF)
    dkn = dk0 - (beta * cd) * ws + mm(dkk, kb) + mm(dkk, kb, 0, 0) + ue
    dk = unit_back(dkn, kn, rk)
    dagram = da * gram
    t = beta * dagram
    s = kn * ue
    dbeta = jnp.sum((dagram + w * z).T, axis=0, keepdims=True)
    dg = dg0 - jnp.sum(t, axis=0, keepdims=True)
    dg = dg + jnp.sum((t - dv * (v.astype(F32) - z) - s).T, axis=0, keepdims=True)
    tail = jnp.sum(s, keepdims=True) + jnp.exp(g_last) * jnp.sum(s0 * e.astype(F32), keepdims=True)
    lane = lax.broadcasted_iota(jnp.int32, (1, c), 1)
    dg = dg + jnp.where(lane == c - 1, tail, 0.0)
    return dv, dk, dg, dbeta


def local_kernel(q, k, v, do, s0, rows, dq, ub, w0, nb, tt, off, z, gram, gs, dk0, dg0):
    for i in range(q.shape[0]):
        outs = local_head(q[i], k[i], v[i], do[i], s0[i], rows[i])
        for ref, value in zip((dq, ub, w0, nb, tt, off, z, gram, gs, dk0, dg0), outs):
            ref[i] = value.astype(ref.dtype)


def carry_kernel(k, v, s0, e, rows, ub, w0, nb, z, gram, gs, dk0, dg0, dv, dk, dg, dbeta):
    for i in range(k.shape[0]):
        outs = carry_head(
            k[i], v[i], s0[i], e[i], rows[i], ub[i], w0[i], nb[i], z[i], gram[i], gs[i], dk0[i], dg0[i]
        )
        for ref, value in zip((dv, dk, dg, dbeta), outs):
            ref[i] = value.astype(ref.dtype)


def chain_kernel(n, tt, off, rows, e_out, inbuf, outbuf, send_sem, recv_sem):
    me = lax.axis_index("seq")
    heads, c = tt.shape[0], rows.shape[2]
    barrier = pltpu.get_barrier_semaphore()
    mesh_id = pl.DeviceIdType.MESH

    @pl.when(me > 0)
    def _():
        pl.semaphore_signal(barrier, inc=1, device_id={"seq": me - 1}, device_id_type=mesh_id)

    @pl.when(me < n - 1)
    def _():
        pl.semaphore_signal(barrier, inc=1, device_id={"seq": me + 1}, device_id_type=mesh_id)

    peers = jnp.where(me > 0, 1, 0) + jnp.where(me < n - 1, 1, 0)
    pl.semaphore_wait(barrier, peers)

    def copy(h):
        return pltpu.make_async_remote_copy(
            src_ref=outbuf.at[h],
            dst_ref=inbuf.at[h],
            send_sem=send_sem.at[h],
            recv_sem=recv_sem.at[h],
            device_id={"seq": me - 1},
            device_id_type=mesh_id,
        )

    @pl.when(me == n - 1)
    def _():
        def first(h, _):
            outbuf[h] = off[h].astype(BF)
            copy(h).start()
            e_out[h] = jnp.zeros(e_out.shape[1:], e_out.dtype)
            return 0

        lax.fori_loop(0, heads, first, 0)

    @pl.when(me < n - 1)
    def _():
        def step(h, _):
            copy(h).wait_recv()
            e = inbuf[h]
            e_out[h] = e

            @pl.when(me > 0)
            def _():
                cdl = jnp.exp(rows[h, 0:1, c - 1 : c])
                outbuf[h] = (off[h] + cdl * e.astype(F32) - mm(tt[h], e)).astype(BF)
                copy(h).start()

            return 0

        lax.fori_loop(0, heads, step, 0)

    @pl.when(me > 0)
    def _():
        def done(h, _):
            copy(h).wait_send()
            return 0

        lax.fori_loop(0, heads, done, 0)


def per_head(kernel, group, ins, outs):
    heads = ins[0].shape[0]

    def spec(a):
        return pl.BlockSpec((group,) + a.shape[1:], lambda h: (h, 0, 0))

    return pl.pallas_call(
        kernel,
        grid=(heads // group,),
        out_shape=outs,
        in_specs=[spec(a) for a in ins],
        out_specs=[spec(a) for a in outs],
        compiler_params=pltpu.CompilerParams(vmem_limit_bytes=48 * 1024 * 1024),
    )(*ins)


def local_part(q, k, v, do, s0, rows):
    h, c, dk = q.shape
    dv = v.shape[2]
    sd = jax.ShapeDtypeStruct
    outs = [
        sd((h, c, dk), BF), sd((h, c, dv), BF), sd((h, c, dv), F32), sd((h, c, dk), BF),
        sd((h, dk, dk), BF), sd((h, dk, dv), F32), sd((h, c, dv), F32), sd((h, c, c), F32),
        sd((h, c, c), F32), sd((h, c, dk), F32), sd((h, 1, c), F32),
    ]
    return per_head(local_kernel, 4, (q, k, v, do, s0, rows), outs)


def carry_part(k, v, s0, e, rows, saved):
    h, c, dk = k.shape
    dv = v.shape[2]
    sd = jax.ShapeDtypeStruct
    outs = [sd((h, c, dv), BF), sd((h, c, dk), BF), sd((h, 1, c), F32), sd((h, 1, c), F32)]
    return per_head(carry_kernel, 4, (k, v, s0, e, rows) + saved, outs)


def chain_part(n, tt, off, rows):
    vm = pl.BlockSpec(memory_space=pltpu.VMEM)
    h = tt.shape[0]
    return pl.pallas_call(
        partial(chain_kernel, n),
        out_shape=jax.ShapeDtypeStruct(off.shape, BF),
        in_specs=[vm] * 3,
        out_specs=vm,
        scratch_shapes=[
            pltpu.VMEM(off.shape, BF),
            pltpu.VMEM(off.shape, BF),
            pltpu.SemaphoreType.DMA((h,)),
            pltpu.SemaphoreType.DMA((h,)),
        ],
        compiler_params=pltpu.CompilerParams(collective_id=0, has_side_effects=True),
    )(tt, off, rows)


def gates(hidden_in, both, decay_bias, decay_log, write_bias):
    h = decay_bias.shape[0]
    logits = lax.dot_general(
        both, hidden_in, (((0,), (1,)), ((), ())), preferred_element_type=F32
    )
    pre = logits[:h] + decay_bias[:, None]
    rate = jnp.exp(decay_log)[:, None]
    beta = jax.nn.sigmoid(logits[h:] + write_bias[:, None])
    log_decay = -rate * jax.nn.softplus(pre)
    c = log_decay.shape[1]
    ones = jnp.triu(jnp.ones((c, c), F32))
    g = jnp.dot(log_decay, ones, precision=HI)
    return pre, rate, beta, g, ones


def shards(
    queries,
    key_vectors,
    values,
    out_grad,
    hidden_in,
    decay_weight,
    write_weight,
    decay_bias,
    decay_log,
    write_bias,
    start_state,
):
    n = lax.axis_size("seq")
    both = jnp.concatenate([decay_weight, write_weight], axis=1)
    pre, rate, beta, g, ones = gates(hidden_in, both, decay_bias, decay_log, write_bias)
    h, c = g.shape
    rows = jnp.concatenate(
        [g[:, None], beta[:, None], jnp.zeros((h, 6, c), F32)], axis=1
    )
    q, k, v, do = (jnp.swapaxes(a, 0, 1) for a in (queries, key_vectors, values, out_grad))
    s0 = start_state[0]
    dq, ub, w0, nb, tt, off, z, gram, gs, dk0, dg0 = local_part(q, k, v, do, s0, rows)
    e = chain_part(n, tt, off, rows)
    dv, dk, dg, dbeta = carry_part(k, v, s0, e, rows, (ub, w0, nb, z, gram, gs, dk0, dg0))
    dlog = jnp.dot(dg[:, 0], ones.T, precision=HI)
    decay_grads = (-dlog * rate * jax.nn.sigmoid(pre)).astype(BF)
    write_grads = (dbeta[:, 0] * beta * (1.0 - beta)).astype(BF)
    grads = jnp.concatenate([decay_grads, write_grads], axis=0)
    weight_terms = jnp.dot(grads, hidden_in, preferred_element_type=F32)
    total = lax.psum(weight_terms, "seq")
    partial_terms = lax.dot_general(
        grads, both, (((0,), (1,)), ((), ())), preferred_element_type=F32
    )
    grad_hidden = lax.psum_scatter(
        partial_terms.astype(BF), "head", scatter_dimension=1, tiled=True
    )
    return (
        jnp.swapaxes(dq, 0, 1),
        jnp.swapaxes(dk, 0, 1),
        jnp.swapaxes(dv, 0, 1),
        grad_hidden,
        total[:h].T,
        total[h:].T,
    )


def solution(mesh):
    placed = (
        P("seq", "head", None),
        P("seq", "head", None),
        P("seq", "head", None),
        P("seq", "head", None),
        P("seq", None),
        P(None, "head"),
        P(None, "head"),
        P("head"),
        P("head"),
        P("head"),
        P("seq", "head", None, None),
    )
    return jax.shard_map(
        shards,
        mesh=mesh,
        in_specs=placed,
        out_specs=(
            P("seq", "head", None),
            P("seq", "head", None),
            P("seq", "head", None),
            P("seq", "head"),
            P(None, "head"),
            P(None, "head"),
        ),
        check_vma=False,
    )
```

time: 822 us -> 249 us (0.30)
  waiting for transfers between devices: 452 us -> 99.1 us
  other arithmetic: 174 us -> 0.26 us
  matrix products: 154 us -> 2.85 us
  Pallas kernels: 0 us -> 112 us
    all_gather x2 -> x0, waiting for transfers between devices: 352 us -> none  [prefix(): gathered = jax.tree.map(lambda a: lax.all_gather(a, axis), part)]
    another operation x7 -> x0, other arithmetic: 160 us -> none  [the longest x4 158 us: block_forward(): jax.scipy.linalg.solve_triangular(unit_lower, right_side, lower=True, uni...]
    dot_general x50 -> x5, matrix products: 140 us -> 2.85 us  [the longest x1 1.14 us: shards(): lax.dot_general(grads, both, (((0,), (1,)), ((), ())), preferred_element_...]
    pallas_call x0 -> x3, Pallas kernels: none -> 112 us  [the longest x1 67 us: chain_part(): pl.pallas_call(partial(chain_kernel, n), out_shape=jax.ShapeDtypeStruct(o...]
    another operation x6 -> x0, matrix products: 14.2 us -> none  [block_forward(): jax.scipy.linalg.solve_triangular(unit_lower, right_side, lower=True, uni...]
    reduce_scatter x1, waiting for transfers between devices: 9.7 us -> 0.01 us  [shards(): lax.psum_scatter(partial_terms.astype(BF), 'head', scatter_dimension=1, t...]
    psum x1, waiting for transfers between devices: 90.5 us -> 99.1 us  [shards(): total = lax.psum(weight_terms, 'seq')]
  transfers between devices with their start and end apart: 4 -> 2, of which waited for: 4 -> 1; matrix products, arithmetic and copies ran while one was open for 6% -> 3% of each run, Pallas kernels for 0% -> 0%
where the time goes in v1:
time: 249 us
  Pallas kernels  112 us (45%)
  waiting for transfers between devices  99.1 us (40%)
  local copies, waits for them, and re-layouts  18.5 us (7%)
  between operations  15.7 us (6%)
  matrix products  2.85 us (1%)
    psum x1, waiting for transfers between devices, shards(): total = lax.psum(weight_terms, 'seq')  99.1 us
    pallas_call x1, Pallas kernels, chain_part(): pl.pallas_call(partial(chain_kernel, n), out_shape=jax.ShapeDtypeStruct(o...  67 us
    pallas_call x2, Pallas kernels, per_head(): pl.pallas_call(kernel, grid=(heads // group,), out_shape=outs, in_specs=[...  45.3 us
    unnamed x48, local copies, waits for them, and re-layouts  14.2 us
  transfers between devices with their start and end apart: 2, of which 1 were waited for; matrix products, arithmetic and copies ran while one was open for 3% of the time, Pallas kernels for 0%

profile of v1, /device:TPU:0, one launch (start us, length us, event | category | flops | bytes accessed | tf_op | source)
XLA Modules:
  0.0 248.7 jit_solution(13550277477839752515)
XLA Ops:
  8.0 0.0 copy-start
  8.0 0.0 copy-start.20
  8.0 0.0 copy-start.16
  8.0 0.0 all-reduce.2.cloned.1.call-start
  8.1 0.6 copy-done.20
  8.7 0.8 constant_dynamic-update-slice_fusion.1
  9.6 0.1 pad.4.clone
  9.7 0.8 constant_dynamic-update-slice_fusion
  10.5 0.0 copy-done
  10.5 0.3 fusion.35
  10.8 0.4 copy-done.19
  11.2 0.1 fusion.17
  11.2 0.0 copy-done.16
  11.2 0.0 copy-start.17
  11.3 0.0 copy-start.18
  11.3 1.4 copy_bitcast_fusion.2
  12.7 0.0 copy-done.17
  12.7 0.3 copy_bitcast_fusion
  13.0 0.0 copy-start.21
  13.0 0.6 copy-done.21
  13.6 0.2 fusion.4
  13.9 0.1 maximum_maximum_fusion.rows
  14.0 35.7 %shard_map.154 = (bf16[16,128,128]{2,1,0:T(8,128)(2,1)S(1)}, bf16[16,128,128]{2,1,0:T(8,128)(2,1)S(1)}, f32[16,128,128]{2,1,0:T(8,128)S(1)}, bf16[16,128,128]{2,...) custom-call(bf16[16,128,128]{2,1,0:T(8,128)(2,1)S(1)} %get-tuple-ele, ...), custom_call_target="tpu_custom_call" | custom-call | tf_op jit(solution)/shard_map/pallas_call | solution.py:197
  49.7 1.0 copy-done.5
  50.7 0.8 copy-done.7
  51.4 0.8 copy-done.9
  52.2 0.8 copy-done.15
  53.0 67.0 %shard_map.155.e = bf16[16,128,128]{2,1,0:T(8,128)(2,1)} custom-call(bf16[16,128,128]{2,1,0:T(8,128)(2,1)} %copy-done.15, f32[16,128,128]{2,1,0:T(8,128)} %get-tuple-element.23.off, f32[16,8,128]{2,1,0:T(8,128)} %copy-done.3), custom_call_target="tpu_custom_call" | custom-call | tf_op jit(solution)/shard_map/pallas_call | solution.py:230
  120.1 1.0 copy-done.2
  121.1 1.2 copy-done.6
  122.3 1.0 copy-done.8
  123.4 9.5 %shard_map.156 = (bf16[16,128,128]{2,1,0:T(8,128)(2,1)S(1)}, bf16[16,128,128]{2,1,0:T(8,128)(2,1)S(1)}, f32[16,1,128]{2,1,0:T(1,128)S(1)}, f32[16,1,128]{2,1,0:T(1,128)S(1)}) custom-call(bf16[16,128,128]{2,1,0:T(8,128)(2,1)S(1)} %get-tuple-element.48.k, bf16[16,128,128]{2,1,0:T(8,128)(2,1)S(1)} %get-tuple-element.47.v, f32[16,128,128]{2,1,0:T(8,128)S(1)} %bitcast.26, ...), custom_call_target="tpu_custom_call" | custom-call | tf_op jit(solution)/shard_map/pallas_call | solution.py:197
  132.9 0.8 copy-done.11
  133.7 0.8 copy-done.13
  134.5 0.1 multiply_convert_fusion
  134.6 0.3 fusion.2
  134.9 0.9 fusion.24
  135.8 0.0 all-reduce.2.cloned.1.call-update
  135.9 0.0 copy-start.10
  135.9 0.0 reduce-scatter.2.cloned.1.call-start
  135.9 1.1 convolution_convert_fusion
  137.1 0.0 reduce-scatter.2.cloned.1.call-update
  137.1 0.0 copy-start.14
  137.1 1.1 copy.21
  138.3 1.1 copy.22
  139.4 1.1 copy.23
  140.5 99.1 %all-reduce.2.cloned.1.call-done = f32[32,2048]{1,0:T(8,128)} async-done(((f32[32,2048]{1,0:T(8,128)}), f32[32,2048]{1,0:T(8,128)}) %all-reduce.2.cloned.1.call-update) | async-done | bytes 262160 | tf_op jit(solution)/shard_map/psum | solution.py:290
  239.6 1.7 slice_bitcast_fusion
  (25 shorter events, 0.0 us)
Async XLA Ops:
  8.0 2.5 %copy-start = (bf16[128,2048]{1,0:T(8,128)(2,1)S(1)}, bf16[128,2048]{1,0:T(8,128)(2,1)}, u32[]{:S(2)}) copy-start(bf16[128,2048]{1,0:T(8,128)(2,1)} %param.15) | copy-start | bytes 1572868
  8.0 0.7 copy-start.20
  8.0 3.2 %copy-start.16 = (bf16[128,16,128]{2,1,0:T(8,128)(2,1)S(1)}, bf16[128,16,128]{2,1,0:T(8,128)(2,1)}, u32[]{:S(2)}) copy-start(bf16[128,16,128]{2,1,0:T(8,128)(2,1)} %param.12) | copy-start | bytes 1572868
  8.0 231.6 %all-reduce.2.cloned.1.call-start = ((), (), s32[]{:S(2)}) async-start(), calls=%async_computation.2 | async-start | bytes 524288 | tf_op jit(solution)/shard_map/psum | solution.py:290
  10.5 0.7 copy-start.19
  11.2 1.4 copy-start.17
  11.3 1.4 copy-start.18
  13.0 0.7 copy-start.21
  14.0 35.7 %copy-start.3 = (f32[16,8,128]{2,1,0:T(8,128)}, f32[16,8,128]{2,1,0:T(8,128)S(1)}, u32[]{:S(2)}) copy-start(f32[16,8,128]{2,1,0:T(8,128)S(1)} %maximum_maximum_fusion.rows) | copy-start | bytes 196612
  49.7 1.0 copy-start.5
  50.6 0.8 copy-start.7
  51.4 0.8 copy-start.9
  52.2 0.8 copy-start.15
  53.0 67.0 %copy-start.1 = (f32[1,16,128,128]{3,2,1,0:T(8,128)S(1)}, f32[1,16,128,128]{3,2,1,0:T(8,128)}, u32[]{:S(2)}) copy-start(f32[1,16,128,128]{3,2,1,0:T(8,128)} %param.21) | copy-start | bytes 3145732
  53.0 67.0 %copy-start.4 = (f32[16,8,128]{2,1,0:T(8,128)S(1)}, f32[16,8,128]{2,1,0:T(8,128)}, u32[]{:S(2)}) copy-start(f32[16,8,128]{2,1,0:T(8,128)} %copy-done.3) | copy-start | bytes 196612
  120.1 1.0 copy-start.2
  121.1 1.2 copy-start.6
  122.3 1.0 copy-start.8
  132.9 0.8 copy-start.11
  133.7 0.8 copy-start.13
  135.9 1.2 copy-start.10
  135.9 105.4 %reduce-scatter.2.cloned.1.call-start = ((), (), s32[]{:S(2)}) async-start(), calls=%async_computation.1 | async-start | bytes 786432 | tf_op jit(solution)/shard_map/reduce_scatter | solution.py:294
  137.1 1.1 copy-start.14
  138.3 1.1 copy-start.12
Sparse Core Ops, SparseCore 0:
  136.0 103.5 all-reduce.1
Sparse Core Ops, SparseCore 1:
  139.2 3.7 reduce-scatter.1

commit v2 on v1

--- a/solution.py
+++ b/solution.py
@@ -34,7 +34,7 @@
     return row, col
 
 
-def local_head(q, k, v, do, s0, rows):
+def local_first(q, k, v, s0, rows):
     c = q.shape[0]
     row, col = indices(c)
     cols = rows.T
@@ -53,13 +53,26 @@
     p = gamma * mm(qb, kb, 1, 1)
     z = v.astype(F32) - cd * mm(kb, sb)
     a = beta * gram
-    inv = jnp.where(row == col, 1.0, jnp.where((row ^ col) == 1, -a, 0.0))
+    return qn, rq, qb, kn, kb, sb, p, z, a, gram, gamma, gamma_strict, beta, cd, to_end
+
+
+def inverses(couplings):
+    c = couplings[0].shape[0]
+    row, col = indices(c)
+    invs = [
+        jnp.where(row == col, 1.0, jnp.where((row ^ col) == 1, -a, 0.0)) for a in couplings
+    ]
     level = 1
     while (2 << level) <= c:
-        low, high = row >> level, col >> level
-        band = jnp.where(((low ^ high) == 1), a, 0.0)
-        inv = inv - mm(mm(inv, band), inv)
+        near = ((row >> level) ^ (col >> level)) == 1
+        halves = [mm(x, jnp.where(near, a, 0.0)) for x, a in zip(invs, couplings)]
+        invs = [x - mm(y, x) for x, y in zip(invs, halves)]
         level += 1
+    return invs
+
+
+def local_rest(do, inv, first):
+    qn, rq, qb, kn, kb, sb, p, z, a, gram, gamma, gamma_strict, beta, cd, to_end = first
     ib = inv.astype(BF)
     ub = mm(ib, beta * z).astype(BF)
     ptdo = mm(p, do, 0, 0)
@@ -110,8 +123,10 @@
 
 
 def local_kernel(q, k, v, do, s0, rows, dq, ub, w0, nb, tt, off, z, gram, gs, dk0, dg0):
+    firsts = [local_first(q[i], k[i], v[i], s0[i], rows[i]) for i in range(q.shape[0])]
+    invs = inverses([first[8] for first in firsts])
     for i in range(q.shape[0]):
-        outs = local_head(q[i], k[i], v[i], do[i], s0[i], rows[i])
+        outs = local_rest(do[i], invs[i], firsts[i])
         for ref, value in zip((dq, ub, w0, nb, tt, off, z, gram, gs, dk0, dg0), outs):
             ref[i] = value.astype(ref.dtype)
 
@@ -167,7 +182,6 @@
         def step(h, _):
             copy(h).wait_recv()
             e = inbuf[h]
-            e_out[h] = e
 
             @pl.when(me > 0)
             def _():
@@ -175,6 +189,7 @@
                 outbuf[h] = (off[h] + cdl * e.astype(F32) - mm(tt[h], e)).astype(BF)
                 copy(h).start()
 
+            e_out[h] = e
             return 0
 
         lax.fori_loop(0, heads, step, 0)
@@ -186,6 +201,120 @@
             return 0
 
         lax.fori_loop(0, heads, done, 0)
+
+
+def sums_kernel(n, m, terms, halves, total, mine, got, part, gathered, got_half, sems, half_sems):
+    me, side = lax.axis_index("seq"), lax.axis_index("head")
+    mesh_id = pl.DeviceIdType.MESH
+    barrier = pltpu.get_barrier_semaphore()
+
+    def greet(d, _):
+        pl.semaphore_signal(
+            barrier, inc=1, device_id={"seq": lax.rem(me + d, n)}, device_id_type=mesh_id
+        )
+        return 0
+
+    def greet_side(d, _):
+        pl.semaphore_signal(
+            barrier, inc=1, device_id={"head": lax.rem(side + d, m)}, device_id_type=mesh_id
+        )
+        return 0
+
+    lax.fori_loop(1, n, greet, 0)
+    lax.fori_loop(1, m, greet_side, 0)
+    pl.semaphore_wait(barrier, n + m - 2)
+
+    def scatter(to, source):
+        return pltpu.make_async_remote_copy(
+            src_ref=terms.at[to], dst_ref=got.at[source],
+            send_sem=sems.at[0, to], recv_sem=sems.at[1, source],
+            device_id={"seq": to}, device_id_type=mesh_id,
+        )
+
+    def gather(to, source):
+        return pltpu.make_async_remote_copy(
+            src_ref=part, dst_ref=gathered.at[source],
+            send_sem=sems.at[2, to], recv_sem=sems.at[3, source],
+            device_id={"seq": to}, device_id_type=mesh_id,
+        )
+
+    def swap(to, source):
+        return pltpu.make_async_remote_copy(
+            src_ref=halves.at[to], dst_ref=got_half.at[source],
+            send_sem=half_sems.at[0, to], recv_sem=half_sems.at[1, source],
+            device_id={"head": to}, device_id_type=mesh_id,
+        )
+
+    def ahead(d):
+        return lax.rem(me + d, n)
+
+    def behind(d):
+        return lax.rem(me + n - d, n)
+
+    def side_ahead(d):
+        return lax.rem(side + d, m)
+
+    def side_behind(d):
+        return lax.rem(side + m - d, m)
+
+    def run(count, body):
+        def step(d, _):
+            body(d)
+            return 0
+
+        lax.fori_loop(1, count, step, 0)
+
+    run(n, lambda d: scatter(ahead(d), me).start())
+    run(m, lambda d: swap(side_ahead(d), side).start())
+
+    def add(d, acc):
+        source = behind(d)
+        scatter(source, source).wait_recv()
+        return acc + got[source]
+
+    acc = lax.fori_loop(1, n, add, terms[me])
+    part[...] = acc
+    total[me] = acc
+    run(n, lambda d: gather(ahead(d), me).start())
+
+    def add_half(d, acc):
+        source = side_behind(d)
+        swap(source, source).wait_recv()
+        return acc + got_half[source].astype(F32)
+
+    mine[...] = lax.fori_loop(1, m, add_half, halves[side].astype(F32)).astype(BF)
+
+    def place(d):
+        source = behind(d)
+        gather(source, source).wait_recv()
+        total[source] = gathered[source]
+
+    run(n, place)
+    run(n, lambda d: scatter(ahead(d), me).wait_send())
+    run(n, lambda d: gather(ahead(d), me).wait_send())
+    run(m, lambda d: swap(side_ahead(d), side).wait_send())
+
+
+def sums_part(n, m, terms, halves):
+    vm = pl.BlockSpec(memory_space=pltpu.VMEM)
+    return pl.pallas_call(
+        partial(sums_kernel, n, m),
+        out_shape=(
+            jax.ShapeDtypeStruct(terms.shape, F32),
+            jax.ShapeDtypeStruct(halves.shape[1:], BF),
+        ),
+        in_specs=[vm] * 2,
+        out_specs=(vm, vm),
+        scratch_shapes=[
+            pltpu.VMEM(terms.shape, F32),
+            pltpu.VMEM(terms.shape[1:], F32),
+            pltpu.VMEM(terms.shape, F32),
+            pltpu.VMEM(halves.shape, BF),
+            pltpu.SemaphoreType.DMA((4, n)),
+            pltpu.SemaphoreType.DMA((2, m)),
+        ],
+        compiler_params=pltpu.CompilerParams(collective_id=1, has_side_effects=True),
+    )(terms, halves)
 
 
 def per_head(kernel, group, ins, outs):
@@ -287,13 +416,17 @@
     write_grads = (dbeta[:, 0] * beta * (1.0 - beta)).astype(BF)
     grads = jnp.concatenate([decay_grads, write_grads], axis=0)
     weight_terms = jnp.dot(grads, hidden_in, preferred_element_type=F32)
-    total = lax.psum(weight_terms, "seq")
-    partial_terms = lax.dot_general(
-        grads, both, (((0,), (1,)), ((), ())), preferred_element_type=F32
-    )
-    grad_hidden = lax.psum_scatter(
-        partial_terms.astype(BF), "head", scatter_dimension=1, tiled=True
-    )
+    width = hidden_in.shape[1]
+    terms = jnp.swapaxes(weight_terms.reshape(2 * h, n, width // n), 0, 1)
+    m = lax.axis_size("head")
+    halves = lax.dot_general(
+        jnp.broadcast_to(grads, (m,) + grads.shape),
+        both.reshape(m, width // m, 2 * h),
+        (((1,), (2,)), ((0,), (0,))),
+        preferred_element_type=F32,
+    ).astype(BF)
+    total, grad_hidden = sums_part(n, m, terms, halves)
+    total = jnp.swapaxes(total, 0, 1).reshape(2 * h, width)
     return (
         jnp.swapaxes(dq, 0, 1),
         jnp.swapaxes(dk, 0, 1),

time: 249 us -> 135 us (0.54)
  waiting for transfers between devices: 99.1 us -> 0 us
  between operations: 15.7 us -> 0.82 us
    psum x1 -> x0, waiting for transfers between devices: 99.1 us -> none  [shards(): total = lax.psum(weight_terms, 'seq')]
    pallas_call x0 -> x1, Pallas kernels: none -> 18.8 us  [sums_part(): pl.pallas_call(partial(sums_kernel, n, m), out_shape=(jax.ShapeDtypeStruc...]
    pallas_call x2, Pallas kernels: 45.3 us -> 28.4 us  [per_head(): pl.pallas_call(kernel, grid=(heads // group,), out_shape=outs, in_specs=[...]
    unnamed x48 -> x44, local copies, waits for them, and re-layouts: 14.2 us -> 13.9 us
  transfers between devices with their start and end apart: 2 -> 0, of which waited for: 1 -> 0; matrix products, arithmetic and copies ran while one was open for 3% -> 0% of each run, Pallas kernels for 0% -> 0%
where the time goes in v2:
time: 135 us; the launch traced here: 134 us
  Pallas kernels  114 us (84%)
  local copies, waits for them, and re-layouts  16.6 us (12%)
  matrix products  2.13 us (2%)
    pallas_call x1, Pallas kernels, chain_part(): pl.pallas_call(partial(chain_kernel, n), out_shape=jax.ShapeDtypeStruct(o...  67 us
    pallas_call x2, Pallas kernels, per_head(): pl.pallas_call(kernel, grid=(heads // group,), out_shape=outs, in_specs=[...  28.4 us
    pallas_call x1, Pallas kernels, sums_part(): pl.pallas_call(partial(sums_kernel, n, m), out_shape=(jax.ShapeDtypeStruc...  18.8 us
    unnamed x44, local copies, waits for them, and re-layouts  13.9 us

profile of v2, /device:TPU:0, one launch (start us, length us, event | category | flops | bytes accessed | tf_op | source)
XLA Modules:
  0.0 134.1 jit_solution(6685960611720241210)
XLA Ops:
  0.6 0.0 copy-start
  0.7 0.0 copy-start.17
  0.7 0.1 pad.4.clone
  0.8 0.6 copy-done.17
  1.4 0.0 copy-start.16
  1.4 0.9 constant_dynamic-update-slice_fusion.1
  2.3 0.0 copy-done.15
  2.3 0.0 copy-start.11
  2.3 0.0 copy-done
  2.3 0.3 fusion.35
  2.6 0.0 copy-done.18
  2.6 0.2 fusion.6
  2.8 0.0 copy-done.16
  2.8 0.1 fusion.19
  2.9 0.1 maximum_maximum_fusion.rows
  3.0 0.3 copy-done.10
  3.3 0.2 copy-done.11
  3.5 0.3 copy_bitcast_fusion.2
  3.8 0.8 copy-done.12
  4.6 0.2 copy-done.13
  4.7 0.3 copy_bitcast_fusion
  5.0 0.0 copy-done.3
  5.0 18.8 %shard_map.154 = (bf16[16,128,128]{2,1,0:T(8,128)(2,1)S(1)}, bf16[16,128,128]{2,1,0:T(8,128)(2,1)S(1)}, f32[16,128,128]{2,1,0:T(8,128)S(1)}, bf16[16,128,128]{2,...) custom-call(bf16[16,128,128]{2,1,0:T(8,128)(2,1)S(1)} %get-tuple-ele, ...), custom_call_target="tpu_custom_call" | custom-call | tf_op jit(solution)/shard_map/pallas_call | solution.py:326
  23.8 1.0 copy-done.5
  24.8 0.8 copy-done.7
  25.6 0.8 copy-done.9
  26.4 1.1 copy.32
  27.5 67.0 %shard_map.155.e = bf16[16,128,128]{2,1,0:T(8,128)(2,1)} custom-call(bf16[16,128,128]{2,1,0:T(8,128)(2,1)} %copy-done.9, f32[16,128,128]{2,1,0:T(8,128)} %get-tuple-element.25.off, f32[16,8,128]{2,1,0:T(8,128)} %copy-done.3), custom_call_target="tpu_custom_call" | custom-call | tf_op jit(solution)/shard_map/pallas_call | solution.py:359
  94.6 0.0 copy-done.1
  94.6 0.0 copy-done.4
  94.6 0.0 copy-start.2
  94.6 1.0 copy-done.2
  95.6 1.2 copy-done.6
  96.8 1.0 copy-done.8
  97.9 9.5 %shard_map.156 = (bf16[16,128,128]{2,1,0:T(8,128)(2,1)S(1)}, bf16[16,128,128]{2,1,0:T(8,128)(2,1)S(1)}, f32[16,1,128]{2,1,0:T(1,128)S(1)}, f32[16,1,128]{2,1,0:T(1,128)S(1)}) custom-call(bf16[16,128,128]{2,1,0:T(8,128)(2,1)S(1)} %get-tuple-element.58.k, bf16[16,128,128]{2,1,0:T(8,128)(2,1)S(1)} %get-tuple-element.57.v, f32[16,128,128]{2,1,0:T(8,128)S(1)} %bitcast.50, ...), custom_call_target="tpu_custom_call" | custom-call | tf_op jit(solution)/shard_map/pallas_call | solution.py:326
  107.4 1.1 copy.33
  108.6 1.1 copy.34
  109.7 0.3 fusion.2
  110.0 0.1 multiply_convert_fusion
  110.1 0.2 convolution_bitcast_fusion
  110.3 0.7 copy.50
  111.0 1.1 convolution_convert_fusion.halves
  112.2 18.8 %shard_map.157 = (f32[16,32,128]{2,1,0:T(8,128)}, bf16[128,1024]{1,0:T(8,128)(2,1)}) custom-call(f32[16,32,128]{2,1,0:T(8,128)} %bitcast.56, bf16[2,128,1024]{2,1,0:T(8,128)(2,1)} %convolution_convert_fusion.halves), custom_call_target="tpu_custom_call" | custom-call | tf_op jit(solution)/shard_map/pallas_call | solution.py:300
  131.0 1.0 slice_bitcast_fusion
  132.0 0.0 copy-start.14
  132.0 0.7 copy.51
  132.7 0.7 copy.52
  133.4 0.7 copy.55
  (19 shorter events, 0.0 us)
Async XLA Ops:
  0.6 1.7 %copy-start = (bf16[128,2048]{1,0:T(8,128)(2,1)S(1)}, bf16[128,2048]{1,0:T(8,128)(2,1)}, u32[]{:S(2)}) copy-start(bf16[128,2048]{1,0:T(8,128)(2,1)} %param.15) | copy-start | bytes 1572868
  0.7 0.7 copy-start.17
  1.4 0.9 copy-start.15
  1.4 1.2 copy-start.18
  1.4 1.5 %copy-start.16 = (f32[16]{0:T(128)S(1)}, f32[16]{0:T(128)}, u32[]{:S(2)}) copy-start(f32[16]{0:T(128)} %param.20) | copy-start | bytes 196
  2.3 1.0 copy-start.10
  2.3 1.2 copy-start.11
  3.5 1.5 %copy-start.3 = (f32[16,8,128]{2,1,0:T(8,128)}, f32[16,8,128]{2,1,0:T(8,128)S(1)}, u32[]{:S(2)}) copy-start(f32[16,8,128]{2,1,0:T(8,128)S(1)} %maximum_maximum_fusion.rows) | copy-start | bytes 196612
  3.5 1.1 copy-start.12
  3.5 1.2 copy-start.13
  23.8 1.0 copy-start.5
  24.8 0.8 copy-start.7
  25.6 0.8 copy-start.9
  27.5 67.0 %copy-start.1 = (f32[1,16,128,128]{3,2,1,0:T(8,128)S(1)}, f32[1,16,128,128]{3,2,1,0:T(8,128)}, u32[]{:S(2)}) copy-start(f32[1,16,128,128]{3,2,1,0:T(8,128)} %param.21) | copy-start | bytes 3145732
  27.5 67.0 %copy-start.4 = (f32[16,8,128]{2,1,0:T(8,128)S(1)}, f32[16,8,128]{2,1,0:T(8,128)}, u32[]{:S(2)}) copy-start(f32[16,8,128]{2,1,0:T(8,128)} %copy-done.3) | copy-start | bytes 196612
  94.6 1.0 copy-start.2
  95.6 1.2 copy-start.6
  96.8 1.0 copy-start.8
  132.0 1.3 %copy-start.14 = (bf16[128,1024]{1,0:T(8,128)(2,1)S(1)}, bf16[128,1024]{1,0:T(8,128)(2,1)}, u32[]{:S(2)}) copy-start(bf16[128,1024]{1,0:T(8,128)(2,1)} %get-tuple-element.69) | copy-start | bytes 786436

commit v3 on v2

--- a/solution.py
+++ b/solution.py
@@ -342,7 +342,7 @@
         sd((h, dk, dk), BF), sd((h, dk, dv), F32), sd((h, c, dv), F32), sd((h, c, c), F32),
         sd((h, c, c), F32), sd((h, c, dk), F32), sd((h, 1, c), F32),
     ]
-    return per_head(local_kernel, 4, (q, k, v, do, s0, rows), outs)
+    return per_head(local_kernel, min(8, h), (q, k, v, do, s0, rows), outs)
 
 
 def carry_part(k, v, s0, e, rows, saved):

time: 135 us -> 131 us (0.970)
  Pallas kernels: 114 us -> 111 us
    pallas_call x2, Pallas kernels: 28.4 us -> 25.2 us  [per_head(): pl.pallas_call(kernel, grid=(heads // group,), out_shape=outs, in_specs=[...]
where the time goes in v3:
time: 131 us
  Pallas kernels  111 us (85%)
  local copies, waits for them, and re-layouts  16.6 us (13%)
  matrix products  2.13 us (2%)
    pallas_call x1, Pallas kernels, chain_part(): pl.pallas_call(partial(chain_kernel, n), out_shape=jax.ShapeDtypeStruct(o...  67 us
    pallas_call x2, Pallas kernels, per_head(): pl.pallas_call(kernel, grid=(heads // group,), out_shape=outs, in_specs=[...  25.2 us
    pallas_call x1, Pallas kernels, sums_part(): pl.pallas_call(partial(sums_kernel, n, m), out_shape=(jax.ShapeDtypeStruc...  18.8 us
    unnamed x44, local copies, waits for them, and re-layouts  13.9 us

profile of v3, /device:TPU:0, one launch (start us, length us, event | category | flops | bytes accessed | tf_op | source)
XLA Modules:
  0.0 130.9 jit_solution(1552650384822115778)
XLA Ops:
  0.6 0.0 copy-start
  0.7 0.0 copy-start.17
  0.7 0.1 pad.4.clone
  0.8 0.6 copy-done.17
  1.4 0.0 copy-start.16
  1.4 0.9 constant_dynamic-update-slice_fusion.1
  2.3 0.0 copy-done.15
  2.3 0.0 copy-start.11
  2.3 0.0 copy-done
  2.3 0.3 fusion.35
  2.6 0.0 copy-done.18
  2.6 0.2 fusion.6
  2.8 0.0 copy-done.16
  2.8 0.1 fusion.19
  2.9 0.1 maximum_maximum_fusion.rows
  3.0 0.3 copy-done.10
  3.3 0.2 copy-done.11
  3.5 0.3 copy_bitcast_fusion.2
  3.8 0.8 copy-done.12
  4.6 0.2 copy-done.13
  4.7 0.3 copy_bitcast_fusion
  5.0 0.0 copy-done.3
  5.0 15.6 %shard_map.154 = (bf16[16,128,128]{2,1,0:T(8,128)(2,1)S(1)}, bf16[16,128,128]{2,1,0:T(8,128)(2,1)S(1)}, f32[16,128,128]{2,1,0:T(8,128)S(1)}, bf16[16,128,128]{2,...) custom-call(bf16[16,128,128]{2,1,0:T(8,128)(2,1)S(1)} %get-tuple-ele, ...), custom_call_target="tpu_custom_call" | custom-call | tf_op jit(solution)/shard_map/pallas_call | solution.py:326
  20.6 1.0 copy-done.5
  21.6 0.8 copy-done.7
  22.4 0.8 copy-done.9
  23.2 1.1 copy.32
  24.3 67.0 %shard_map.155.e = bf16[16,128,128]{2,1,0:T(8,128)(2,1)} custom-call(bf16[16,128,128]{2,1,0:T(8,128)(2,1)} %copy-done.9, f32[16,128,128]{2,1,0:T(8,128)} %get-tuple-element.25.off, f32[16,8,128]{2,1,0:T(8,128)} %copy-done.3), custom_call_target="tpu_custom_call" | custom-call | tf_op jit(solution)/shard_map/pallas_call | solution.py:359
  91.3 0.0 copy-done.1
  91.3 0.0 copy-done.4
  91.4 0.0 copy-start.2
  91.4 1.0 copy-done.2
  92.4 1.2 copy-done.6
  93.6 1.0 copy-done.8
  94.7 9.5 %shard_map.156 = (bf16[16,128,128]{2,1,0:T(8,128)(2,1)S(1)}, bf16[16,128,128]{2,1,0:T(8,128)(2,1)S(1)}, f32[16,1,128]{2,1,0:T(1,128)S(1)}, f32[16,1,128]{2,1,0:T(1,128)S(1)}) custom-call(bf16[16,128,128]{2,1,0:T(8,128)(2,1)S(1)} %get-tuple-element.58.k, bf16[16,128,128]{2,1,0:T(8,128)(2,1)S(1)} %get-tuple-element.57.v, f32[16,128,128]{2,1,0:T(8,128)S(1)} %bitcast.50, ...), custom_call_target="tpu_custom_call" | custom-call | tf_op jit(solution)/shard_map/pallas_call | solution.py:326
  104.2 1.1 copy.33
  105.4 1.1 copy.34
  106.5 0.3 fusion.2
  106.8 0.1 multiply_convert_fusion
  106.9 0.2 convolution_bitcast_fusion
  107.1 0.7 copy.50
  107.8 1.1 convolution_convert_fusion.halves
  109.0 18.8 %shard_map.157 = (f32[16,32,128]{2,1,0:T(8,128)}, bf16[128,1024]{1,0:T(8,128)(2,1)}) custom-call(f32[16,32,128]{2,1,0:T(8,128)} %bitcast.56, bf16[2,128,1024]{2,1,0:T(8,128)(2,1)} %convolution_convert_fusion.halves), custom_call_target="tpu_custom_call" | custom-call | tf_op jit(solution)/shard_map/pallas_call | solution.py:300
  127.8 1.0 slice_bitcast_fusion
  128.8 0.0 copy-start.14
  128.8 0.7 copy.51
  129.5 0.7 copy.52
  130.2 0.7 copy.55
  (19 shorter events, 0.0 us)
Async XLA Ops:
  0.6 1.7 %copy-start = (bf16[128,2048]{1,0:T(8,128)(2,1)S(1)}, bf16[128,2048]{1,0:T(8,128)(2,1)}, u32[]{:S(2)}) copy-start(bf16[128,2048]{1,0:T(8,128)(2,1)} %param.15) | copy-start | bytes 1572868
  0.7 0.7 copy-start.17
  1.4 0.9 copy-start.15
  1.4 1.2 copy-start.18
  1.4 1.5 %copy-start.16 = (f32[16]{0:T(128)S(1)}, f32[16]{0:T(128)}, u32[]{:S(2)}) copy-start(f32[16]{0:T(128)} %param.20) | copy-start | bytes 196
  2.3 1.0 copy-start.10
  2.3 1.2 copy-start.11
  3.5 1.5 %copy-start.3 = (f32[16,8,128]{2,1,0:T(8,128)}, f32[16,8,128]{2,1,0:T(8,128)S(1)}, u32[]{:S(2)}) copy-start(f32[16,8,128]{2,1,0:T(8,128)S(1)} %maximum_maximum_fusion.rows) | copy-start | bytes 196612
  3.5 1.1 copy-start.12
  3.5 1.2 copy-start.13
  20.6 1.0 copy-start.5
  21.6 0.8 copy-start.7
  22.4 0.8 copy-start.9
  24.3 67.0 %copy-start.1 = (f32[1,16,128,128]{3,2,1,0:T(8,128)S(1)}, f32[1,16,128,128]{3,2,1,0:T(8,128)}, u32[]{:S(2)}) copy-start(f32[1,16,128,128]{3,2,1,0:T(8,128)} %param.21) | copy-start | bytes 3145732
  24.3 67.0 %copy-start.4 = (f32[16,8,128]{2,1,0:T(8,128)S(1)}, f32[16,8,128]{2,1,0:T(8,128)}, u32[]{:S(2)}) copy-start(f32[16,8,128]{2,1,0:T(8,128)} %copy-done.3) | copy-start | bytes 196612
  91.4 1.0 copy-start.2
  92.4 1.2 copy-start.6
  93.6 1.0 copy-start.8
  128.8 1.3 %copy-start.14 = (bf16[128,1024]{1,0:T(8,128)(2,1)S(1)}, bf16[128,1024]{1,0:T(8,128)(2,1)}, u32[]{:S(2)}) copy-start(bf16[128,1024]{1,0:T(8,128)(2,1)} %get-tuple-element.69) | copy-start | bytes 786436
